TPU v7x, 512 devices: a whole 4x8x8 slice. The times are simulated.
512 devices in a mesh: dp: 2 (over core), ctx: 64 (over z, y), head: 4 (over x).
Axes of the slice: x: 4, y: 8, z: 8, core: 2. Of those that a mesh axis runs over, the one named last changes fastest.
Arguments:
- queries: bfloat16 [2, 8192, 2560], P('dp', 'ctx', 'head'), may hold values from -25 to 25
- keys: bfloat16 [2, 8192, 2560], P('dp', 'ctx', 'head'), may hold values from -25 to 25
- values: bfloat16 [2, 8192, 2560], P('dp', 'ctx', 'head'), may hold values from -6 to 6
- grad_y: bfloat16 [2, 8192, 2560], P('dp', 'ctx', 'head'), may hold values from -6 to 6
- out_gain: float32 [2560], P('head'), may hold values from 0.1 to 1.9
- offsets: int32 [2, 20], P(None, 'head'), may hold values from 0 to 63, as said below
Outputs:
- attended: bfloat16 [2, 8192, 2560], P('dp', 'ctx', 'head')
- query_grad: bfloat16 [2, 8192, 2560], P('dp', 'ctx', 'head')
- key_grad: bfloat16 [2, 8192, 2560], P('dp', 'ctx', 'head')
- value_grad: bfloat16 [2, 8192, 2560], P('dp', 'ctx', 'head')
- gain_grad: float32 [2560], P('head')
Inputs may be any that keep to these rules, and one draw needn't show every extreme that they name: Row 0 holds offsets below 8, row 1 offsets below 64.
All inputs are finite; a program needn't handle non-finite values.
Results may differ from a plain program's by a relative error of at most 0.011.
Values may be sent and summed in bfloat16 or wider, within the bound.
A program may use at most 64 MiB of HBM per device.

v0:
```python
import math
import jax
import jax.numpy as jnp
from jax import lax
from jax.sharding import PartitionSpec as P

HEAD_DIM = 128
SPAN = 4
R1 = 8
EPS = 1e-06


def group_gather(block, axis, group):
    count = lax.axis_size(axis)
    pieces = [block]
    for shift in range(1, group):
        route = []
        for src in range(count):
            base = src - src % group
            route.append((src, base + (src % group + shift) % group))
        pieces.append(lax.ppermute(block, axis, route))
    return jnp.concatenate(pieces, 0)


def pick_rows(source_rows, dilation, shifts):
    row_count, head_count, head_width = source_rows.shape
    grouped = source_rows.reshape(row_count // dilation, dilation, head_count, head_width)
    hit_mask = jnp.arange(dilation, dtype=jnp.int32).reshape(1, dilation, 1, 1) == shifts.reshape(
        1, 1, head_count, 1
    )
    chosen = jnp.where(hit_mask, grouped, jnp.zeros((), source_rows.dtype))
    return jnp.sum(chosen, axis=1, dtype=source_rows.dtype)


def place_rows(row_values, dilation, shifts):
    row_count, head_count, head_width = row_values.shape
    hit_mask = jnp.arange(dilation, dtype=jnp.int32).reshape(1, dilation, 1, 1) == shifts.reshape(
        1, 1, head_count, 1
    )
    spread = jnp.where(hit_mask, row_values[:, None], jnp.zeros((), row_values.dtype))
    return spread.reshape(row_count * dilation, head_count, head_width)


def level_scores(q_rows, k_rows):
    score_scale = 1.0 / math.sqrt(q_rows.shape[-1])
    return (
        jnp.einsum("qhe,khe->hqk", q_rows, k_rows, preferred_element_type=jnp.float32) * score_scale
    )


def attend(q_rows, k_rows, v_rows):
    scores = level_scores(q_rows, k_rows)
    row_max = jnp.max(scores, axis=-1, keepdims=True)
    log_total = row_max[..., 0] + jnp.log(jnp.sum(jnp.exp(scores - row_max), axis=-1))
    soft_rows = jnp.exp(scores - log_total[..., None]).astype(jnp.bfloat16)
    level_out = jnp.einsum("hqk,khe->qhe", soft_rows, v_rows, preferred_element_type=jnp.float32)
    return (level_out, log_total.T)


def score_grads(q_rows, k_rows, v_rows, log_total, grad_low, row_shift):
    score_scale = 1.0 / math.sqrt(q_rows.shape[-1])
    scores = level_scores(q_rows, k_rows)
    exact_soft = jnp.exp(scores - log_total.T[..., None])
    prob_grad = jnp.einsum("qhe,khe->hqk", grad_low, v_rows, preferred_element_type=jnp.float32)
    score_grad = (exact_soft * (prob_grad + row_shift.T[..., None]) * score_scale).astype(
        jnp.bfloat16
    )
    return (score_grad, exact_soft.astype(jnp.bfloat16))


def key_parts(score_grad, soft_low, q_rows, grad_low):
    k_part = jnp.einsum("hqk,qhe->khe", score_grad, q_rows, preferred_element_type=jnp.float32)
    v_part = jnp.einsum("hqk,qhe->khe", soft_low, grad_low, preferred_element_type=jnp.float32)
    return (k_part, v_part)


def query_part(score_grad, k_rows):
    return jnp.einsum("hqk,khe->qhe", score_grad, k_rows, preferred_element_type=jnp.float32)


def split_qkv(packed, head_count):
    width = head_count * HEAD_DIM
    shape = (packed.shape[0], head_count, HEAD_DIM)
    return tuple((packed[:, i * width : (i + 1) * width].reshape(shape) for i in range(3)))


def pack_grads(grad_low, row_shift):
    rows = grad_low.shape[0]
    return jnp.concatenate(
        [grad_low.astype(jnp.float32).reshape(rows, -1), row_shift.astype(jnp.float32)], 1
    )


def unpack_grads(packed, head_count):
    width = head_count * HEAD_DIM
    grad_low = packed[:, :width].astype(jnp.bfloat16).reshape(-1, head_count, HEAD_DIM)
    return (grad_low, packed[:, width:])


def shards(queries, keys, values, grad_y, out_gain, offsets):
    tokens = queries.shape[1]
    flat_width = queries.shape[2]
    head_count = flat_width // HEAD_DIM
    row_shape = (tokens, head_count, HEAD_DIM)
    q_own = queries[0].reshape(row_shape)
    k_own = keys[0].reshape(row_shape)
    v_own = values[0].reshape(row_shape)
    ctx_size = lax.axis_size("ctx")
    my_place = lax.axis_index("ctx")
    mid_shift = offsets[0]
    top_shift = offsets[1]
    positions = jnp.arange(tokens, dtype=jnp.int32)
    mid_hit = (positions % R1)[:, None] == mid_shift[None, :]
    top_hit = (positions % ctx_size)[:, None] == top_shift[None, :]
    mid_pack = jnp.concatenate(
        [pick_rows(x, R1, mid_shift).reshape(-1, flat_width) for x in (q_own, k_own, v_own)], 1
    )
    top_pack = jnp.concatenate(
        [pick_rows(x, ctx_size, top_shift).reshape(-1, flat_width) for x in (q_own, k_own, v_own)],
        1,
    )
    mid_rows = mid_pack.shape[0]
    top_rows = top_pack.shape[0]
    mid_all = group_gather(mid_pack, "ctx", SPAN)
    top_all = lax.all_gather(top_pack, "ctx", axis=0, tiled=True)
    mid_q, mid_k, mid_v = split_qkv(mid_all, head_count)
    top_q, top_k, top_v = split_qkv(top_all, head_count)
    top_start = my_place * top_rows
    base_out, base_total = attend(q_own, k_own, v_own)
    mid_out_all, mid_total_all = attend(mid_q, mid_k, mid_v)
    top_out_all, top_total_all = attend(top_q, top_k, top_v)
    mid_out = mid_out_all[:mid_rows]
    mid_total = mid_total_all[:mid_rows]
    top_out = lax.dynamic_slice_in_dim(top_out_all, top_start, top_rows, 0)
    top_total = lax.dynamic_slice_in_dim(top_total_all, top_start, top_rows, 0)
    mid_full = place_rows(mid_total[..., None], R1, mid_shift)[..., 0]
    top_full = place_rows(top_total[..., None], ctx_size, top_shift)[..., 0]
    row_max = jnp.maximum(base_total, jnp.where(mid_hit, mid_full, base_total))
    row_max = jnp.maximum(row_max, jnp.where(top_hit, top_full, base_total))
    base_expo = jnp.exp(base_total - row_max)
    mid_expo = jnp.where(mid_hit, jnp.exp(mid_full - row_max), 0.0)
    top_expo = jnp.where(top_hit, jnp.exp(top_full - row_max), 0.0)
    denom = base_expo + mid_expo + top_expo
    base_share = base_expo / denom
    mid_share = mid_expo / denom
    top_share = top_expo / denom
    attn = (
        base_share[..., None] * base_out
        + mid_share[..., None] * place_rows(mid_out, R1, mid_shift)
        + top_share[..., None] * place_rows(top_out, ctx_size, top_shift)
    )
    inv_rms = lax.rsqrt(jnp.mean(attn * attn, axis=-1, keepdims=True) + EPS)
    normed = attn * inv_rms
    gain_rows = out_gain.reshape(head_count, HEAD_DIM)
    attended = (normed * gain_rows).astype(jnp.bfloat16).reshape(1, tokens, flat_width)
    grad_full = grad_y[0].reshape(row_shape).astype(jnp.float32)
    gain_part = jnp.sum(grad_full * normed, axis=0).reshape(flat_width)
    gain_grad = lax.psum(gain_part, ("dp", "ctx"))
    grad_norm = grad_full * gain_rows
    grad_attn = inv_rms * (
        grad_norm - normed * jnp.mean(grad_norm * normed, axis=-1, keepdims=True)
    )
    inner = jnp.sum(grad_attn * attn, axis=-1)
    base_low = (base_share[..., None] * grad_attn).astype(jnp.bfloat16)
    base_shift = -(base_share * inner)
    base_grad, base_soft = score_grads(q_own, k_own, v_own, base_total, base_low, base_shift)
    base_dq = query_part(base_grad, k_own)
    base_dk, base_dv = key_parts(base_grad, base_soft, q_own, base_low)
    mid_sel = pick_rows(mid_share[..., None], R1, mid_shift)[..., 0]
    mid_low = (mid_sel[..., None] * pick_rows(grad_attn, R1, mid_shift)).astype(jnp.bfloat16)
    mid_row_shift = -(mid_sel * pick_rows(inner[..., None], R1, mid_shift)[..., 0])
    top_sel = pick_rows(top_share[..., None], ctx_size, top_shift)[..., 0]
    top_low = (top_sel[..., None] * pick_rows(grad_attn, ctx_size, top_shift)).astype(jnp.bfloat16)
    top_row_shift = -(top_sel * pick_rows(inner[..., None], ctx_size, top_shift)[..., 0])
    mid_low_all, mid_shift_all = unpack_grads(
        group_gather(pack_grads(mid_low, mid_row_shift), "ctx", SPAN), head_count
    )
    top_low_all, top_shift_all = unpack_grads(
        lax.all_gather(pack_grads(top_low, top_row_shift), "ctx", axis=0, tiled=True), head_count
    )
    mid_grad, mid_soft = score_grads(mid_q, mid_k, mid_v, mid_total_all, mid_low_all, mid_shift_all)
    mid_dq = query_part(mid_grad[:, :mid_rows], mid_k)
    mid_dk, mid_dv = key_parts(
        mid_grad[:, :, :mid_rows], mid_soft[:, :, :mid_rows], mid_q, mid_low_all
    )
    top_grad, top_soft = score_grads(top_q, top_k, top_v, top_total_all, top_low_all, top_shift_all)
    own_grad = lax.dynamic_slice_in_dim(top_grad, top_start, top_rows, 1)
    top_dq = query_part(own_grad, top_k)
    key_grad_cols = lax.dynamic_slice_in_dim(top_grad, top_start, top_rows, 2)
    key_soft_cols = lax.dynamic_slice_in_dim(top_soft, top_start, top_rows, 2)
    top_dk, top_dv = key_parts(key_grad_cols, key_soft_cols, top_q, top_low_all)
    query_grad = (
        base_dq + place_rows(mid_dq, R1, mid_shift) + place_rows(top_dq, ctx_size, top_shift)
    )
    key_grad = base_dk + place_rows(mid_dk, R1, mid_shift) + place_rows(top_dk, ctx_size, top_shift)
    value_grad = (
        base_dv + place_rows(mid_dv, R1, mid_shift) + place_rows(top_dv, ctx_size, top_shift)
    )
    out_shape = (1, tokens, flat_width)
    return (
        attended,
        query_grad.astype(jnp.bfloat16).reshape(out_shape),
        key_grad.astype(jnp.bfloat16).reshape(out_shape),
        value_grad.astype(jnp.bfloat16).reshape(out_shape),
        gain_grad,
    )


def solution(mesh):
    in_specs = (
        P("dp", "ctx", "head"),
        P("dp", "ctx", "head"),
        P("dp", "ctx", "head"),
        P("dp", "ctx", "head"),
        P("head"),
        P(None, "head"),
    )
    out_specs = (
        P("dp", "ctx", "head"),
        P("dp", "ctx", "head"),
        P("dp", "ctx", "head"),
        P("dp", "ctx", "head"),
        P("head"),
    )
    return jax.shard_map(shards, mesh=mesh, in_specs=in_specs, out_specs=out_specs, check_vma=False)
```

profile of v0, /device:TPU:256, one launch (start us, length us, event | category | flops | bytes accessed | tf_op | source)
XLA Modules:
  0.0 428.5 jit_solution(14037007713612233846)
XLA Ops:
  0.6 0.8 slice_bitcast_fusion.5
  1.4 0.6 copy-done.23
  2.0 1.5 fusion.24
  3.6 5.5 %collective-permute-start.2 = (bf16[16,1920]{1,0:T(8,128)(2,1)S(1)}, bf16[16,1920]{1,0:T(8,128)(2,1)S(1)}, u32[]{:S(2)}, u32[]{:S(2)}) collective-permute-start(bf16[16,1920]{1,0:T(8,128)(2,1)S(1)} %bitcast_dynamic-update-slice_fusion), channel_id=1, source_target_pairs={{0,12},{4,0},{8,4},{12,8},{16,28},{20,16},{24,20},{28,24},{32,44},... | collective-permute-start | bytes 184328 | tf_op jit(solution)/shard_map/ppermute | solution.py:21
  9.1 1.9 collective-permute-start.1
  11.0 2.9 collective-permute-start
  14.1 0.7 copy-done.1
  15.1 0.7 copy-done.2
  16.8 0.4 copy-done.21
  17.2 0.7 broadcast_in_dim.285
  17.9 0.6 broadcast_in_dim.278
  18.9 0.3 select_reduce_fusion.2
  19.2 50.0 %all-gather = bf16[64,2,1920]{2,1,0:T(2,128)(2,1)S(1)} all-gather(bf16[1,2,1920]{2,1,0:T(2,128)(2,1)S(1)} %maximum_bitcast_fusion.1), channel_id=1, replica_groups=mesh['dp'=2,'ctx'=64,'head'=4] {'ctx'}, dimensions={0}, use_global_device_ids=true | all-gather | bytes 499200 | tf_op jit(solution)/shard_map/all_gather | solution.py:125
  69.9 0.3 fusion.67
  70.4 0.5 copy-done.7
  71.0 0.7 broadcast_in_dim.289
  72.0 0.3 fusion.69
  72.8 0.5 copy-done.9
  73.8 0.4 copy-done.19
  74.9 0.5 multiply_reduce_fusion.3
  75.5 0.7 copy-done.13
  76.1 0.8 multiply_reduce_fusion
  76.9 0.7 copy-done.15
  78.0 0.6 negate_bitcast_fusion
  79.1 0.6 pad_maximum_fusion.2
  79.7 2.6 collective-permute-start.5
  82.3 3.1 collective-permute-start.4
  85.4 2.3 collective-permute-start.3
  88.0 0.4 copy-done.22
  88.7 49.2 %all-gather.1 = f32[64,2,645]{2,1,0:T(2,128)S(1)} all-gather(f32[1,2,645]{2,1,0:T(2,128)S(1)} %maximum_bitcast_fusion.2), channel_id=1, replica_groups=mesh['dp'=2,'ctx'=64,'head'=4] {'ctx'}, dimensions={0}, use_global_device_ids=true | all-gather | bytes 335400 | tf_op jit(solution)/shard_map/all_gather | solution.py:179
  137.9 0.3 reshape.372
  138.2 0.7 slice.99
  138.9 0.4 fusion.17
  139.3 0.5 copy-done.3
  140.1 0.5 copy-done.8
  141.1 0.4 convolution_bitcast_fusion.8
  141.7 0.8 copy.357
  142.7 0.5 copy-done.17
  143.2 277.9 %psum.7 = f32[640]{0:T(1024)} all-reduce(f32[640]{0:T(1024)S(1)} %bitcast.273), channel_id=1, replica_groups=mesh['dp'=2,'ctx'=64,'head'=4] {'dp','ctx'}, use_global_device_ids=true, to_apply=%region_22.23 | all-reduce | flops 640 | bytes 5120 | tf_op jit(solution)/shard_map/psum | solution.py:158
  421.1 0.9 pad_maximum_fusion.1
  422.1 0.8 maximum_bitcast_fusion
  423.0 0.5 copy-done.10
  424.1 0.6 copy-done.12
  425.1 0.8 copy.359
  426.0 0.3 fusion.13
  426.4 0.8 copy.358
  427.2 0.3 fusion.15
  427.7 0.8 copy.360
  (128 shorter events, 8.9 us)
Async XLA Ops:
  1.4 0.6 copy-start.23
  1.4 15.2 %copy-start.25 = (s32[5]{0:T(128)}, s32[5]{0:T(128)S(1)}, u32[]{:S(2)}) copy-start(s32[5]{0:T(128)S(1)} %get-tuple-element.62) | copy-start | bytes 64
  2.0 15.9 %copy-start.14 = (pred[8,5]{0,1:T(8,128)(4,1)}, pred[8,5]{0,1:T(8,128)(4,1)S(1)}, u32[]{:S(2)}) copy-start(pred[8,5]{0,1:T(8,128)(4,1)S(1)} %iota_compare_fusion.1) | copy-start | bytes 124
  2.0 11.9 %copy-start = (bf16[1,128,640]{2,1,0:T(8,128)(2,1)S(1)}, bf16[1,128,640]{2,1,0:T(8,128)(2,1)}, u32[]{:S(2)}) copy-start(bf16[1,128,640]{2,1,0:T(8,128)(2,1)} %param.6) | copy-start | bytes 491524
  3.6 68.8 %collective-permute-start.2 = (bf16[16,1920]{1,0:T(8,128)(2,1)S(1)}, bf16[16,1920]{1,0:T(8,128)(2,1)S(1)}, u32[]{:S(2)}, u32[]{:S(2)}) collective-permute-start(bf16[16,1920]{1,0:T(8,128)(2,1)S(1)} %bitcast_dynamic-update-slice_fusion), channel_id=1, source_target_pairs={{0,12},{4,0},{8,4},{12,8},{16,28},{20,16},{24,20},{28,24},{32,44},... | collective-permute-start | bytes 184328 | tf_op jit(solution)/shard_map/ppermute | solution.py:21
  9.1 63.3 %collective-permute-start.1 = (bf16[16,1920]{1,0:T(8,128)(2,1)S(1)}, bf16[16,1920]{1,0:T(8,128)(2,1)S(1)}, u32[]{:S(2)}, u32[]{:S(2)}) collective-permute-start(bf16[16,1920]{1,0:T(8,128)(2,1)S(1)} %bitcast_dynamic-update-slice_fusion), channel_id=1, source_target_pairs={{0,8},{4,12},{8,0},{12,4},{16,24},{20,28},{24,16},{28,20},{32,40},... | collective-permute-start | bytes 184328 | tf_op jit(solution)/shard_map/ppermute | solution.py:21
  11.0 61.3 %collective-permute-start = (bf16[16,1920]{1,0:T(8,128)(2,1)S(1)}, bf16[16,1920]{1,0:T(8,128)(2,1)S(1)}, u32[]{:S(2)}, u32[]{:S(2)}) collective-permute-start(bf16[16,1920]{1,0:T(8,128)(2,1)S(1)} %bitcast_dynamic-update-slice_fusion), channel_id=1, source_target_pairs={{0,4},{4,8},{8,12},{12,0},{16,20},{20,24},{24,28},{28,16},{32,36},... | collective-permute-start | bytes 184328 | tf_op jit(solution)/shard_map/ppermute | solution.py:21
  14.0 0.9 copy-start.1
  14.9 0.9 copy-start.2
  16.4 2.2 copy-start.6
  16.7 0.5 copy-start.21
  70.3 0.6 copy-start.7
  72.4 1.0 copy-start.4
  72.7 0.6 copy-start.9
  73.5 0.7 copy-start.19
  73.5 0.7 copy-start.26
  73.7 0.7 copy-start.18
  73.7 0.7 copy-start.11
  73.8 0.7 copy-start.24
  75.4 0.7 copy-start.13
  76.9 0.7 copy-start.15
  79.7 341.3 %collective-permute-start.5 = (f32[16,645]{1,0:T(8,128)}, f32[16,645]{1,0:T(8,128)}, u32[]{:S(2)}, u32[]{:S(2)}) collective-permute-start(f32[16,645]{1,0:T(8,128)} %pad_maximum_fusion.2), channel_id=1, source_target_pairs={{0,12},{4,0},{8,4},{12,8},{16,28},{20,16},{24,20},{28,24},{32,44},... | collective-permute-start | bytes 123848 | tf_op jit(solution)/shard_map/ppermute | solution.py:21
  82.3 338.8 %collective-permute-start.4 = (f32[16,645]{1,0:T(8,128)}, f32[16,645]{1,0:T(8,128)}, u32[]{:S(2)}, u32[]{:S(2)}) collective-permute-start(f32[16,645]{1,0:T(8,128)} %pad_maximum_fusion.2), channel_id=1, source_target_pairs={{0,8},{4,12},{8,0},{12,4},{16,24},{20,28},{24,16},{28,20},{32,40},... | collective-permute-start | bytes 123848 | tf_op jit(solution)/shard_map/ppermute | solution.py:21
  85.4 335.7 %collective-permute-start.3 = (f32[16,645]{1,0:T(8,128)}, f32[16,645]{1,0:T(8,128)}, u32[]{:S(2)}, u32[]{:S(2)}) collective-permute-start(f32[16,645]{1,0:T(8,128)} %pad_maximum_fusion.2), channel_id=1, source_target_pairs={{0,4},{4,8},{8,12},{12,0},{16,20},{20,24},{24,28},{28,16},{32,36},... | collective-permute-start | bytes 123848 | tf_op jit(solution)/shard_map/ppermute | solution.py:21
  87.7 0.6 copy-start.22
  138.2 0.7 copy-start.16
  138.9 0.9 copy-start.3
  140.0 0.7 copy-start.8
  141.7 0.8 copy-start.20
  142.5 0.7 copy-start.17
  422.1 0.9 copy-start.5
  422.8 0.7 copy-start.10
  424.1 0.6 copy-start.12
where the time goes:
time: 429 us
  blocking collectives  377 us (88%)
  local copies, waits for them, and re-layouts  19.9 us (5%)
  starting transfers between devices  18.3 us (4%)
  other arithmetic  7.42 us (2%)
  matrix products  4.56 us (1%)
    psum x1, blocking collectives, shards(): gain_grad = lax.psum(gain_part, ('dp', 'ctx'))  278 us
    all_gather x1, blocking collectives, shards(): top_all = lax.all_gather(top_pack, 'ctx', axis=0, tiled=True)  50 us
    all_gather x1, blocking collectives, shards(): lax.all_gather(pack_grads(top_low, top_row_shift), 'ctx', axis=0, tiled=T...  49.2 us
    ppermute x6, starting transfers between devices, group_gather(): pieces.append(lax.ppermute(block, axis, route))  18.3 us
    unnamed x69, local copies, waits for them, and re-layouts  13.1 us
  transfers between devices with their start and end apart: 6, of which 0 were waited for; matrix products, arithmetic and copies ran while one was open for 2% of the time, Pallas kernels for 0%

commit v1 on v0

--- a/solution.py
+++ b/solution.py
@@ -8,6 +8,12 @@
 SPAN = 4
 R1 = 8
 EPS = 1e-06
+
+
+def gather_from_all(x, axis, dim):
+    devices = lax.axis_size(axis)
+    repeats = [devices if d == dim else 1 for d in range(x.ndim)]
+    return lax.all_to_all(jnp.tile(x, repeats), axis, split_axis=dim, concat_axis=dim, tiled=True)
 
 
 def group_gather(block, axis, group):
@@ -176,7 +182,7 @@
         group_gather(pack_grads(mid_low, mid_row_shift), "ctx", SPAN), head_count
     )
     top_low_all, top_shift_all = unpack_grads(
-        lax.all_gather(pack_grads(top_low, top_row_shift), "ctx", axis=0, tiled=True), head_count
+        gather_from_all(pack_grads(top_low, top_row_shift), "ctx", 0), head_count
     )
     mid_grad, mid_soft = score_grads(mid_q, mid_k, mid_v, mid_total_all, mid_low_all, mid_shift_all)
     mid_dq = query_part(mid_grad[:, :mid_rows], mid_k)

time: 429 us -> 386 us (0.90)
  the two profiles are of different devices: /device:TPU:256 before, /device:TPU:258 now
where the time goes in v1:
time: 386 us; the launch traced here: 385 us
  blocking collectives  328 us (85%)
  starting transfers between devices  30.3 us (8%)
  local copies, waits for them, and re-layouts  15.9 us (4%)
  other arithmetic  5.21 us (1%)
  matrix products  4.57 us (1%)
    psum x1, blocking collectives, shards(): gain_grad = lax.psum(gain_part, ('dp', 'ctx'))  278 us
    all_gather x1, blocking collectives, shards(): top_all = lax.all_gather(top_pack, 'ctx', axis=0, tiled=True)  50 us
    ppermute x6, starting transfers between devices, group_gather(): pieces.append(lax.ppermute(block, axis, route))  18.3 us
    all_to_all x1, starting transfers between devices, gather_from_all(): lax.all_to_all(jnp.tile(x, repeats), axis, split_axis=dim, concat_axis=di...  12 us
    unnamed x54, local copies, waits for them, and re-layouts  10.3 us
  transfers between devices with their start and end apart: 7, of which 0 were waited for; matrix products, arithmetic and copies ran while one was open for 2% of the time, Pallas kernels for 0%

profile of v1, /device:TPU:258, one launch (start us, length us, event | category | flops | bytes accessed | tf_op | source)
XLA Modules:
  0.0 385.3 jit_solution(10244286904732172255)
XLA Ops:
  0.6 0.8 slice_bitcast_fusion.5
  1.5 1.5 fusion.24
  3.0 5.5 %collective-permute-start.2 = (bf16[16,1920]{1,0:T(8,128)(2,1)S(1)}, bf16[16,1920]{1,0:T(8,128)(2,1)S(1)}, u32[]{:S(2)}, u32[]{:S(2)}) collective-permute-start(bf16[16,1920]{1,0:T(8,128)(2,1)S(1)} %bitcast_dynamic-update-slice_fusion), channel_id=1, source_target_pairs={{0,12},{4,0},{8,4},{12,8},{16,28},{20,16},{24,20},{28,24},{32,44},... | collective-permute-start | bytes 184328 | tf_op jit(solution)/shard_map/ppermute | solution.py:27
  8.5 1.9 collective-permute-start.1
  10.5 2.9 collective-permute-start
  13.6 0.7 copy-done.1
  14.5 0.7 copy-done.2
  15.4 0.2 reshape_reshape_squeeze.21
  15.6 0.2 reshape_reshape_squeeze.22
  16.2 0.4 copy-done.18
  17.2 0.3 select_reduce_fusion.2
  17.5 50.0 %all-gather = bf16[64,2,1920]{2,1,0:T(2,128)(2,1)S(1)} all-gather(bf16[1,2,1920]{2,1,0:T(2,128)(2,1)S(1)} %maximum_bitcast_fusion.1), channel_id=1, replica_groups=mesh['dp'=2,'ctx'=64,'head'=4] {'ctx'}, dimensions={0}, use_global_device_ids=true | all-gather | bytes 499200 | tf_op jit(solution)/shard_map/all_gather | solution.py:131
  68.3 0.3 fusion.67
  68.7 0.5 copy-done.8
  69.5 0.3 fusion.70
  69.8 0.3 fusion.69
  70.5 0.5 copy-done.10
  71.2 0.2 convolution_bitcast_fusion.4
  71.7 0.2 fusion.20
  72.0 0.5 multiply_reduce_fusion.3
  72.5 0.7 copy-done.14
  73.2 0.8 multiply_reduce_fusion
  74.0 0.3 fusion.19
  74.9 0.6 pad_maximum_fusion.2
  75.5 2.6 collective-permute-start.5
  78.1 3.1 collective-permute-start.4
  81.2 2.3 collective-permute-start.3
  83.5 0.2 fusion.18
  83.8 0.4 fusion.17
  84.2 0.3 copy-done.19
  85.0 0.8 copy.357
  85.8 0.8 tile.2
  86.7 12.0 %all-to-all-start = ((f32[64,2,645]{2,1,0:T(2,128)}), f32[64,2,645]{2,1,0:T(2,128)S(1)}, u32[]{:S(2)}, u32[]{:S(2)}) async-start(f32[64,2,645]{2,1,0:T(2,128)} %tile.2), calls=%async_computation | async-start | bytes 786432 | tf_op jit(solution)/shard_map/all_to_all | solution.py:16
  98.7 278.1 %psum.7 = f32[640]{0:T(1024)} all-reduce(f32[640]{0:T(1024)S(1)} %bitcast.271), channel_id=1, replica_groups=mesh['dp'=2,'ctx'=64,'head'=4] {'dp','ctx'}, use_global_device_ids=true, to_apply=%region_22.23 | all-reduce | flops 640 | bytes 5120 | tf_op jit(solution)/shard_map/psum | solution.py:164
  376.9 0.7 copy-done.11
  378.0 0.2 convolution_bitcast_fusion.7
  378.2 0.3 all_to_all.7
  379.0 0.5 copy-done.9
  379.5 0.3 fusion.16
  380.0 0.4 convolution_bitcast_fusion.8
  380.3 0.3 copy-done.17
  380.9 0.7 copy-done.13
  381.5 0.2 fusion.14
  381.9 0.8 copy.359
  382.8 0.3 fusion.13
  383.2 0.8 copy.358
  384.0 0.3 fusion.15
  384.5 0.8 copy.360
  (116 shorter events, 6.5 us)
Async XLA Ops:
  1.5 11.9 %copy-start = (bf16[1,128,640]{2,1,0:T(8,128)(2,1)S(1)}, bf16[1,128,640]{2,1,0:T(8,128)(2,1)}, u32[]{:S(2)}) copy-start(bf16[1,128,640]{2,1,0:T(8,128)(2,1)} %param.6) | copy-start | bytes 491524
  3.0 67.1 %collective-permute-start.2 = (bf16[16,1920]{1,0:T(8,128)(2,1)S(1)}, bf16[16,1920]{1,0:T(8,128)(2,1)S(1)}, u32[]{:S(2)}, u32[]{:S(2)}) collective-permute-start(bf16[16,1920]{1,0:T(8,128)(2,1)S(1)} %bitcast_dynamic-update-slice_fusion), channel_id=1, source_target_pairs={{0,12},{4,0},{8,4},{12,8},{16,28},{20,16},{24,20},{28,24},{32,44},... | collective-permute-start | bytes 184328 | tf_op jit(solution)/shard_map/ppermute | solution.py:27
  8.5 61.6 %collective-permute-start.1 = (bf16[16,1920]{1,0:T(8,128)(2,1)S(1)}, bf16[16,1920]{1,0:T(8,128)(2,1)S(1)}, u32[]{:S(2)}, u32[]{:S(2)}) collective-permute-start(bf16[16,1920]{1,0:T(8,128)(2,1)S(1)} %bitcast_dynamic-update-slice_fusion), channel_id=1, source_target_pairs={{0,8},{4,12},{8,0},{12,4},{16,24},{20,28},{24,16},{28,20},{32,40},... | collective-permute-start | bytes 184328 | tf_op jit(solution)/shard_map/ppermute | solution.py:27
  10.5 59.7 %collective-permute-start = (bf16[16,1920]{1,0:T(8,128)(2,1)S(1)}, bf16[16,1920]{1,0:T(8,128)(2,1)S(1)}, u32[]{:S(2)}, u32[]{:S(2)}) collective-permute-start(bf16[16,1920]{1,0:T(8,128)(2,1)S(1)} %bitcast_dynamic-update-slice_fusion), channel_id=1, source_target_pairs={{0,4},{4,8},{8,12},{12,0},{16,20},{20,24},{24,28},{28,16},{32,36},... | collective-permute-start | bytes 184328 | tf_op jit(solution)/shard_map/ppermute | solution.py:27
  13.4 0.9 copy-start.1
  14.3 0.9 copy-start.2
  15.8 1.1 copy-start.3
  16.1 0.6 copy-start.18
  16.8 55.0 %copy-start.16 = (pred[128,5]{0,1:T(8,128)(4,1)}, pred[128,5]{0,1:T(8,128)(4,1)S(1)}, u32[]{:S(2)}) copy-start(pred[128,5]{0,1:T(8,128)(4,1)S(1)} %broadcast_in_dim.285) | copy-start | bytes 1924
  16.9 55.1 %copy-start.12 = (pred[128,5]{0,1:T(8,128)(4,1)}, pred[128,5]{0,1:T(8,128)(4,1)S(1)}, u32[]{:S(2)}) copy-start(pred[128,5]{0,1:T(8,128)(4,1)S(1)} %broadcast_in_dim.278) | copy-start | bytes 1924
  68.6 0.6 copy-start.8
  70.4 0.6 copy-start.10
  71.5 12.2 %copy-start.4 = (f32[128,5]{0,1:T(8,128)}, f32[128,5]{0,1:T(8,128)S(1)}, u32[]{:S(2)}) copy-start(f32[128,5]{0,1:T(8,128)S(1)} %get-tuple-element.44) | copy-start | bytes 7684
  71.5 12.2 %copy-start.6 = (f32[5,128]{1,0:T(8,128)}, f32[5,128]{1,0:T(8,128)S(1)}, u32[]{:S(2)}) copy-start(f32[5,128]{1,0:T(8,128)S(1)} %get-tuple-element.48) | copy-start | bytes 7684
  72.5 0.7 copy-start.14
  75.5 301.3 %collective-permute-start.5 = (f32[16,645]{1,0:T(8,128)}, f32[16,645]{1,0:T(8,128)S(1)}, u32[]{:S(2)}, u32[]{:S(2)}) collective-permute-start(f32[16,645]{1,0:T(8,128)} %pad_maximum_fusion.2), channel_id=1, source_target_pairs={{0,12},{4,0},{8,4},{12,8},{16,28},{20,16},{24,20},{28,24},{32,44},... | collective-permute-start | bytes 123848 | tf_op jit(solution)/shard_map/ppermute | solution.py:27
  78.1 298.7 %collective-permute-start.4 = (f32[16,645]{1,0:T(8,128)}, f32[16,645]{1,0:T(8,128)S(1)}, u32[]{:S(2)}, u32[]{:S(2)}) collective-permute-start(f32[16,645]{1,0:T(8,128)} %pad_maximum_fusion.2), channel_id=1, source_target_pairs={{0,8},{4,12},{8,0},{12,4},{16,24},{20,28},{24,16},{28,20},{32,40},... | collective-permute-start | bytes 123848 | tf_op jit(solution)/shard_map/ppermute | solution.py:27
  81.2 295.6 %collective-permute-start.3 = (f32[16,645]{1,0:T(8,128)}, f32[16,645]{1,0:T(8,128)S(1)}, u32[]{:S(2)}, u32[]{:S(2)}) collective-permute-start(f32[16,645]{1,0:T(8,128)} %pad_maximum_fusion.2), channel_id=1, source_target_pairs={{0,4},{4,8},{8,12},{12,0},{16,20},{20,24},{24,28},{28,16},{32,36},... | collective-permute-start | bytes 123848 | tf_op jit(solution)/shard_map/ppermute | solution.py:27
  83.8 0.7 copy-start.19
  86.7 12.0 %copy-start.15 = (f32[5,128]{1,0:T(8,128)S(1)}, f32[5,128]{1,0:T(8,128)}, u32[]{:S(2)}) copy-start(f32[5,128]{1,0:T(8,128)} %get-tuple-element.30) | copy-start | bytes 7684
  86.7 291.5 %all-to-all-start = ((f32[64,2,645]{2,1,0:T(2,128)}), f32[64,2,645]{2,1,0:T(2,128)S(1)}, u32[]{:S(2)}, u32[]{:S(2)}) async-start(f32[64,2,645]{2,1,0:T(2,128)} %tile.2), calls=%async_computation | async-start | bytes 786432 | tf_op jit(solution)/shard_map/all_to_all | solution.py:16
  376.9 0.7 copy-start.11
  378.8 0.7 copy-start.9
  380.0 0.7 copy-start.17
  380.8 0.7 copy-start.13
  383.2 0.8 copy-start.5
  383.2 0.8 copy-start.7
